TPU v7x, 32 devices: a whole 2x2x4 slice. The times are simulated.
32 devices in a mesh: pipe: 4 (over x, core), expert: 4 (over z), pair: 2 (over y).
Axes of the slice: x: 2, y: 2, z: 4, core: 2. Of those that a mesh axis runs over, the one named last changes fastest.
Arguments:
- tokens: bfloat16 [4096, 2048], P(('pipe', 'expert')), may hold values from -8 to 8
- expert_ids: int32 [4096, 2], P(('pipe', 'expert')), may hold values from 0 to 3, all different within a row; in each aligned block of 256 rows (0 to 255, 256 to 511, ...) at most 256 rows name the same one
- block_mask: int32 [32, 8], P(('pipe', 'expert')), may hold values from 0 to 1, as said below
- attn_gain: float32 [4, 2048], P('pipe'), may hold values from 0.1 to 1.9
- w_qkv: bfloat16 [4, 2048, 8, 384], P('pipe', None, 'pair'), may hold values from -3 to 3
- w_out: bfloat16 [4, 8, 128, 2048], P('pipe', 'pair'), may hold values from -4 to 4
- moe_gain: float32 [4, 2048], P('pipe'), may hold values from 0.1 to 1.9
- w_router: bfloat16 [4, 2048, 4], P('pipe'), may hold values from -0.125 to 0.125
- w_up: bfloat16 [4, 4, 2048, 3584], P('pipe', 'expert', None, 'pair'), may hold values from -0.125 to 0.125
- w_down: bfloat16 [4, 4, 3584, 2048], P('pipe', 'expert', 'pair'), may hold values from -0.09375 to 0.09375
Outputs:
- next_input: bfloat16 [4096, 2048], P(('pipe', 'expert'))
Inputs may be any that keep to these rules, and one draw needn't show every extreme that they name: `expert_ids`: in each aligned block of 256 rows (the rows of one device) no expert is named by more than 256 rows. `block_mask`: entry [b, c] is 1 where query block b may attend to key block c of its own micro-batch; every block attends to itself.
All inputs are finite; a program needn't handle non-finite values.
Results may differ from a plain program's by a relative error of at most 0.0095.
Values may be sent and summed in bfloat16 or wider, within the bound.
No kernel may reach another device: no remote copies, remote signals or barrier semaphores. Data moves between devices by JAX's collectives and lax.ppermute only.
A program may use at most 128 MiB of HBM per device.

v0:
```python
import jax
import jax.numpy as jnp
from jax import lax
from jax.sharding import PartitionSpec as P

BLOCK = 128


def passed_along(value, axis, steps):
    count = lax.axis_size(axis)
    pairs = [(source, (source + steps) % count) for source in range(count)]
    return lax.ppermute(value, axis, pairs)


def rms_scale(values, gain):
    widened = values.astype(jnp.float32)
    return widened * lax.rsqrt(jnp.mean(widened * widened, axis=-1, keepdims=True) + 1e-05) * gain


def pair_total(partial_term):
    return lax.psum(partial_term.astype(jnp.bfloat16), "pair").astype(jnp.float32)


def local(
    tokens, expert_ids, block_mask, attn_gain, w_qkv, w_out, moe_gain, w_router, w_up, w_down
):
    rows_here = tokens.shape[0]
    model_width = tokens.shape[1]
    heads_here = w_qkv.shape[2]
    head_dim = w_qkv.shape[3] // 3
    block_count = block_mask.shape[1]
    normed = rms_scale(tokens, attn_gain[0]).astype(jnp.bfloat16)
    projected = jnp.einsum(
        "td,dhc->thc", normed, w_qkv[0], preferred_element_type=jnp.float32
    ).astype(jnp.bfloat16)
    queries = projected[:, :, :head_dim]
    key_rows = projected[:, :, head_dim : 2 * head_dim]
    value_rows = projected[:, :, 2 * head_dim :]
    mask_local = block_mask.astype(jnp.float32)
    score_scale = head_dim ** (-0.5)
    start_max = jnp.full((heads_here, rows_here), -1e30, jnp.float32)
    row_max = start_max
    shard_keys = lax.all_gather(key_rows, "expert", axis=0, tiled=True)
    shard_values = lax.all_gather(value_rows, "expert", axis=0, tiled=True)
    shard_rows = shard_keys.shape[0]
    scores = (
        jnp.einsum("qhc,khc->hqk", queries, shard_keys, preferred_element_type=jnp.float32)
        * score_scale
    )
    key_block = jnp.arange(shard_rows, dtype=jnp.int32) // BLOCK
    selector = (key_block[:, None] == jnp.arange(block_count, dtype=jnp.int32)[None, :]).astype(
        jnp.float32
    )
    allowed_blocks = jnp.dot(mask_local, jnp.transpose(selector))
    allowed = jnp.repeat(allowed_blocks, BLOCK, axis=0)[None] > 0.5
    masked = jnp.where(allowed, scores, -1e30)
    new_max = jnp.maximum(row_max, jnp.max(masked, axis=-1))
    weights = jnp.where(allowed, jnp.exp(masked - new_max[:, :, None]), 0.0)
    denominator = jnp.sum(weights, axis=-1)
    numerator = jnp.einsum(
        "hqk,khc->qhc",
        weights.astype(jnp.bfloat16),
        shard_values,
        preferred_element_type=jnp.float32,
    )
    row_max, denominator, numerator = (new_max, denominator, numerator)
    attended = (numerator / jnp.transpose(denominator)[:, :, None]).astype(jnp.bfloat16)
    mixed = jnp.einsum("thc,hcd->td", attended, w_out[0], preferred_element_type=jnp.float32)
    residual = tokens.astype(jnp.float32) + pair_total(mixed)
    moe_in = rms_scale(residual, moe_gain[0]).astype(jnp.bfloat16)
    logits = jnp.dot(moe_in, w_router[0], preferred_element_type=jnp.float32)
    expert_count = logits.shape[1]
    picks_top = expert_ids.shape[1]
    one_hot = expert_ids[:, :, None] == jnp.arange(expert_count, dtype=jnp.int32)[None, None, :]
    chosen = jnp.sum(jnp.where(one_hot, logits[:, None, :], 0.0), axis=-1)
    gate_values = jax.nn.sigmoid(chosen)
    mix_weights = gate_values / jnp.sum(gate_values, axis=1, keepdims=True)
    copy_hits = one_hot.reshape(rows_here * picks_top, expert_count).astype(jnp.int32)
    position = jnp.sum((jnp.cumsum(copy_hits, axis=0) - 1) * copy_hits, axis=1)
    counts = jnp.sum(copy_hits, axis=0)
    capacity = min(rows_here, 2 * rows_here * picks_top // expert_count)
    flat_slot = expert_ids.reshape(-1) * capacity + position
    source_copy = (
        jnp.zeros((expert_count * capacity,), jnp.int32)
        .at[flat_slot]
        .set(jnp.arange(1, rows_here * picks_top + 1, dtype=jnp.int32))
    )
    filled = source_copy > 0
    taken = jnp.take(moe_in, jnp.maximum(source_copy - 1, 0) // picks_top, axis=0)
    outgoing = jnp.where(filled[:, None], taken, jnp.zeros((), jnp.bfloat16)).reshape(
        expert_count, capacity, model_width
    )
    count_column = counts.reshape(expert_count, 1)
    arrived, arrived_counts = (
        lax.all_to_all(outgoing, "expert", split_axis=0, concat_axis=0, tiled=True),
        lax.all_to_all(count_column, "expert", split_axis=0, concat_axis=0, tiled=True),
    )
    sources = arrived.shape[0]
    slot_total = sources * capacity
    flat_rows = arrived.reshape(slot_total, model_width)
    up_weight = w_up[0, 0]
    down_weight = w_down[0, 0]
    lifted = jnp.dot(flat_rows, up_weight, preferred_element_type=jnp.float32)
    hidden = jax.nn.gelu(lifted, approximate=True).astype(jnp.bfloat16)
    partial_out = jnp.dot(hidden, down_weight, preferred_element_type=jnp.float32)
    partial_out = partial_out.reshape(sources, capacity, model_width)
    summed = pair_total(partial_out).astype(jnp.bfloat16)
    back = lax.all_to_all(summed, "expert", split_axis=0, concat_axis=0, tiled=True)
    back_rows = back.reshape(expert_count * capacity, model_width)
    returned = jnp.take(back_rows, flat_slot, axis=0).reshape(rows_here, picks_top, model_width)
    layer_out = (
        residual + jnp.sum(mix_weights[:, :, None] * returned.astype(jnp.float32), axis=1)
    ).astype(jnp.bfloat16)
    return passed_along(layer_out, "pipe", 1)


def solution(mesh):
    return jax.shard_map(
        local,
        mesh=mesh,
        in_specs=(
            P(("pipe", "expert"), None),
            P(("pipe", "expert"), None),
            P(("pipe", "expert"), None),
            P("pipe", None),
            P("pipe", None, "pair", None),
            P("pipe", "pair", None, None),
            P("pipe", None),
            P("pipe", None, None),
            P("pipe", "expert", None, "pair"),
            P("pipe", "expert", "pair", None),
        ),
        out_specs=P(("pipe", "expert"), None),
        check_vma=False,
    )
```

profile of v0, /device:TPU:0, one launch (start us, length us, event | category | flops | bytes accessed | tf_op | source)
XLA Modules:
  0.0 496.8 jit_solution(15261917762017467929)
XLA Ops:
  6.5 1.7 fusion.23
  8.2 5.0 %fusion.30 = bf16[256,4,384]{2,0,1:T(8,128)(2,1)S(1)} fusion(bf16[2048,4,384]{2,1,0:T(4,128)(2,1)} %bitcast.80, bf16[256,2048]{1,0:T(8,128)(2,1)} %param.10, f32[2048]{0:T(1024)} %bitcast.81, f32[256]{0:T(256)S(1)} %add_rsqrt_fusion.1), kind=kOutput, calls=%fused_computation.41 | convolution fusion | flops 1613103104 | bytes 8135680 | tf_op jit(solution)/shard_map/td,dhc->thc/dot_general | solution.py:33
  13.2 0.9 fusion.71
  14.2 0.0 all-gather.3.cloned.1.call-start
  14.2 0.7 all-gather.3.cloned.1.call-update
  15.0 0.1 copy.32
  15.1 0.1 eq.52
  15.3 1.2 reduce-window.6
  16.5 0.8 slice_reduce_fusion
  17.3 0.6 broadcast_multiply_fusion
  17.9 0.3 fusion.36
  18.2 26.8 %all-gather.5.cloned.1.call-done = bf16[1024,4,128]{2,0,1:T(8,128)(2,1)} async-done(((bf16[256,4,128]{2,0,1:T(8,128)(2,1)}), bf16[1024,4,128]{2,0,1:T(8,128)(2,1)}) %all-gather.5.cloned.1.call-update) | async-done | bytes 1048592 | tf_op jit(solution)/shard_map/all_gather | solution.py:43
  45.0 0.1 broadcast_in_dim.87
  45.1 2.2 fusion.19
  47.3 1.9 copy-done.3
  49.2 2.1 fusion.20
  51.4 22.6 %all-gather.3.cloned.1.call-done = bf16[1024,4,128]{2,0,1:T(8,128)(2,1)} async-done(((bf16[256,4,128]{2,0,1:T(8,128)(2,1)}), bf16[1024,4,128]{2,0,1:T(8,128)(2,1)}) %all-gather.3.cloned.1.call-update) | async-done | bytes 1048592 | tf_op jit(solution)/shard_map/all_gather | solution.py:44
  74.0 5.5 %fusion.22 = bf16[256,2048]{1,0:T(8,128)(2,1)} fusion(bf16[1,4,128,2048]{3,2,1,0:T(8,128)(2,1)S(1)} %copy-done, bf16[1024,4,128]{2,0,1:T(8,128)(2,1)} %all-gather.3.cloned.1.call-done, f32[4,256,1024]{2,1,0:T(8,128)} %copy-done.3, f32[4,256]{1,0:T(4,128)S(1)} %broadcast_maximum_fusion, pred[256,1024]{1,0:T(8,128)(4,1)S(1)} %bitcast.71, f32[256,4]{0,1:T(4,128)} %bitcast.77), kind=kOutput, calls=%fused_computation.31 | convolution fusion | flops 811335680 | bytes 8658944 | tf_op jit(solution)/shard_map/thc,hcd->td/dot_general | solution.py:68
  79.5 0.0 all-reduce.5.cloned.1.call-start
  79.6 0.1 reshape.155
  79.7 0.8 copy.36
  80.5 0.1 mul.117
  80.6 0.8 reduce-window.9
  81.5 0.1 add_bitcast_fusion
  81.6 2.4 scatter_custom_fusion
  84.1 35.0 %all-reduce.3.cloned.1.call-done = bf16[256,2048]{1,0:T(8,128)(2,1)} async-done(((bf16[256,2048]{1,0:T(8,128)(2,1)}), bf16[256,2048]{1,0:T(8,128)(2,1)}) %all-reduce.3.cloned.1.call-update) | async-done | bytes 1048592 | tf_op jit(solution)/shard_map/psum | solution.py:21
  119.1 1.6 multiply_reduce_fusion.1
  120.8 1.8 multiply_convert_fusion
  122.5 6.0 %gather_fusion = bf16[1024,2048]{1,0:T(8,128)(2,1)} fusion(bf16[256,2048]{1,0:T(8,128)(2,1)S(1)} %multiply_convert_fusion, s32[1024]{0:T(1024)S(1)} %broadcast_clamp_fusion), kind=kCustom, calls=%fused_computation | custom fusion | bytes 8392704 | tf_op jit(solution)/shard_map/jit(_take)/gather | solution.py:89
  128.6 2.6 select_select_fusion
  131.2 97.6 %all_to_all.10 = bf16[4,256,2048]{2,1,0:T(8,128)(2,1)S(1)} all-to-all(bf16[4,256,2048]{2,1,0:T(8,128)(2,1)S(1)} %select_select_fusion), channel_id=1, replica_groups=mesh['pipe'=4,'expert'=4,'pair'=2] {'expert'}, dimensions={0} | all-to-all | bytes 8388608 | tf_op jit(solution)/shard_map/all_to_all | solution.py:95
  228.8 12.1 %fusion.7 = bf16[1024,1792]{1,0:T(8,128)(2,1)S(1)} fusion(bf16[1024,2048]{1,0:T(8,128)(2,1)S(1)} %bitcast.68, bf16[1,1,2048,1792]{3,2,1,0:T(8,128)(2,1)} %param.18), kind=kOutput, calls=%fused_computation.11 | convolution fusion | flops 7532707840 | bytes 15204352 | tf_op jit(solution)/shard_map/dot_general | solution.py:103
  240.9 9.3 %fusion.16 = bf16[4,256,2048]{2,1,0:T(8,128)(2,1)} fusion(bf16[4,256,1792]{2,1,0:T(8,128)(2,1)S(1)} %bitcast.82, bf16[1,1,1792,2048]{3,2,1,0:T(8,128)(2,1)S(1)} %bitcast.79), kind=kOutput, calls=%fused_computation.23 | convolution fusion | flops 7518289920 | bytes 15204352 | tf_op jit(solution)/shard_map/dot_general | solution.py:105
  250.3 106.2 %all-reduce.5.cloned.1.call-done = bf16[4,256,2048]{2,1,0:T(8,128)(2,1)} async-done(((bf16[4,256,2048]{2,1,0:T(8,128)(2,1)}), bf16[4,256,2048]{2,1,0:T(8,128)(2,1)}) %all-reduce.5.cloned.1.call-update) | async-done | bytes 4194320 | tf_op jit(solution)/shard_map/psum | solution.py:21
  356.5 5.1 %all-to-all-start.1 = ((bf16[4,256,2048]{2,1,0:T(8,128)(2,1)}), bf16[4,256,2048]{2,1,0:T(8,128)(2,1)}, u32[]{:S(2)}, u32[]{:S(2)}) async-start(bf16[4,256,2048]{2,1,0:T(8,128)(2,1)} %all-reduce.5.cloned.1.call-done), calls=%async_computation.1 | async-start | bytes 8388608 | tf_op jit(solution)/shard_map/all_to_all | solution.py:108
  361.5 0.1 reduce_sum.73
  361.7 0.1 copy.34
  361.8 0.2 copy.35
  362.0 0.4 fusion.53
  362.5 0.1 copy.31
  362.6 92.1 %all-to-all-done.1 = bf16[4,256,2048]{2,1,0:T(8,128)(2,1)} async-done(((bf16[4,256,2048]{2,1,0:T(8,128)(2,1)}), bf16[4,256,2048]{2,1,0:T(8,128)(2,1)}, u32[]{:S(2)}, u32[]{:S(2)}) %all-to-all-start.1) | async-done | bytes 4194336 | tf_op jit(solution)/shard_map/all_to_all | solution.py:108
  454.7 7.1 %gather_fusion.1 = bf16[512,2048]{1,0:T(8,128)(2,1)S(1)} fusion(bf16[1024,2048]{1,0:T(8,128)(2,1)} %bitcast.20, s32[1024]{0:T(1024)S(1)} %pad_clamp_fusion), kind=kCustom, calls=%fused_computation.1 | custom fusion | bytes 4196352 | tf_op jit(solution)/shard_map/jit(_take)/gather | solution.py:110
  461.8 2.7 gather.15
  464.5 10.1 %multiply_reduce_fusion = f32[256,2048]{1,0:T(8,128)S(1)} fusion(bf16[256,2,2048]{2,1,0:T(2,128)(2,1)} %gather.15, pred[256,2]{1,0:T(8,128)(4,1)S(1)} %copy.35, f32[256,2]{1,0:T(8,128)S(1)} %copy.31), kind=kLoop, calls=%fused_computation.18 | loop fusion | flops 3670016 | bytes 4196864 | tf_op jit(solution)/shard_map/reduce_sum | solution.py:112
  474.5 0.5 add_convert_fusion
  475.1 0.1 collective-permute-start
  475.1 14.2 %collective-permute-done = bf16[256,2048]{1,0:T(8,128)(2,1)S(1)} collective-permute-done((bf16[256,2048]{1,0:T(8,128)(2,1)S(1)}, bf16[256,2048]{1,0:T(8,128)(2,1)S(1)}, u32[]{:S(2)}, u32[]{:S(2)}) %collective-permute-start) | collective-permute-done | bytes 1048608 | tf_op jit(solution)/shard_map/ppermute | solution.py:12
  489.3 1.0 copy.48
  (42 shorter events, 0.3 us)
Async XLA Ops:
  6.5 67.5 %copy-start = (bf16[1,4,128,2048]{3,2,1,0:T(8,128)(2,1)S(1)}, bf16[1,4,128,2048]{3,2,1,0:T(8,128)(2,1)}, u32[]{:S(2)}) copy-start(bf16[1,4,128,2048]{3,2,1,0:T(8,128)(2,1)} %param.15) | copy-start | bytes 6291460
  6.5 38.5 %all-gather.5.cloned.1.call-start = ((), (), s32[]{:S(2)}) async-start(), calls=%async_computation.3 | async-start | bytes 1310720 | tf_op jit(solution)/shard_map/all_gather | solution.py:43
  8.2 6.8 %copy-start.5 = (s32[256,2]{0,1:T(2,128)S(1)}, s32[256,2]{0,1:T(2,128)}, u32[]{:S(2)}) copy-start(s32[256,2]{0,1:T(2,128)} %param.11) | copy-start | bytes 6148
  8.2 9.7 %copy-start.7 = (s32[2,8]{1,0:T(2,128)S(1)}, s32[2,8]{1,0:T(2,128)}, u32[]{:S(2)}) copy-start(s32[2,8]{1,0:T(2,128)} %param.12) | copy-start | bytes 196
  14.2 59.8 %all-gather.3.cloned.1.call-start = ((), (), s32[]{:S(2)}) async-start(), calls=%async_computation.2 | async-start | bytes 1310720 | tf_op jit(solution)/shard_map/all_gather | solution.py:44
  14.9 104.2 %all-reduce.3.cloned.1.call-start = ((), (), s32[]{:S(2)}) async-start(), calls=%async_computation.4 | async-start | bytes 2097152 | tf_op jit(solution)/shard_map/psum | solution.py:21
  47.3 1.9 copy-start.3
  74.0 45.1 %copy-start.2 = (bf16[256,2048]{1,0:T(8,128)(2,1)S(1)}, bf16[256,2048]{1,0:T(8,128)(2,1)}, u32[]{:S(2)}) copy-start(bf16[256,2048]{1,0:T(8,128)(2,1)} %param.10) | copy-start | bytes 3145732
  79.5 277.0 %all-reduce.5.cloned.1.call-start = ((), (), s32[]{:S(2)}) async-start(), calls=%async_computation.5 | async-start | bytes 8388608 | tf_op jit(solution)/shard_map/psum | solution.py:21
  131.1 109.8 %slice-start = ((s8[7340032]{0:T(1024)(128)(4,1)}), s8[4194304]{0:T(1024)(128)(4,1)S(1)}, s32[]{:S(2)}) async-start(s8[7340032]{0:T(1024)(128)(4,1)} %bitcast.78), calls=%async_computation.6 | async-start | bytes 8388608
  228.8 12.1 %slice-start.1 = ((s8[7340032]{0:T(1024)(128)(4,1)}), s8[3145728]{0:T(1024)(128)(4,1)S(1)}, s32[]{:S(2)}) async-start(s8[7340032]{0:T(1024)(128)(4,1)} %bitcast.78), calls=%async_computation.7 | async-start | bytes 6291456
  250.3 111.7 %copy-start.6 = (bf16[1,2048,4]{1,2,0:T(4,128)(2,1)S(1)}, bf16[1,2048,4]{1,2,0:T(4,128)(2,1)}, u32[]{:S(2)}) copy-start(bf16[1,2048,4]{1,2,0:T(4,128)(2,1)} %param.17) | copy-start | bytes 49156
  356.5 98.2 %all-to-all-start.1 = ((bf16[4,256,2048]{2,1,0:T(8,128)(2,1)}), bf16[4,256,2048]{2,1,0:T(8,128)(2,1)}, u32[]{:S(2)}, u32[]{:S(2)}) async-start(bf16[4,256,2048]{2,1,0:T(8,128)(2,1)} %all-reduce.5.cloned.1.call-done), calls=%async_computation.1 | async-start | bytes 8388608 | tf_op jit(solution)/shard_map/all_to_all | solution.py:108
  464.5 10.1 %copy-start.4 = (bf16[256,2048]{1,0:T(8,128)(2,1)S(1)}, bf16[256,2048]{1,0:T(8,128)(2,1)}, u32[]{:S(2)}) copy-start(bf16[256,2048]{1,0:T(8,128)(2,1)} %all-reduce.3.cloned.1.call-done) | copy-start | bytes 3145732
  464.5 25.8 %copy-start.1 = (bf16[1,4,128,2048]{3,2,1,0:T(8,128)(2,1)S(1)}, bf16[1,4,128,2048]{3,2,1,0:T(8,128)(2,1)}, u32[]{:S(2)}) copy-start(bf16[1,4,128,2048]{3,2,1,0:T(8,128)(2,1)} %param.15) | copy-start | bytes 6291460
  475.1 14.3 %collective-permute-start = (bf16[256,2048]{1,0:T(8,128)(2,1)S(1)}, bf16[256,2048]{1,0:T(8,128)(2,1)S(1)}, u32[]{:S(2)}, u32[]{:S(2)}) collective-permute-start(bf16[256,2048]{1,0:T(8,128)(2,1)S(1)} %add_convert_fusion), channel_id=1, source_target_pairs={{0,8},{8,16},{16,24},{24,0},{1,9},{9,17},{17,25},{25,1},{2,10},{10... | collective-permute-start | bytes 3145736 | tf_op jit(solution)/shard_map/ppermute | solution.py:12
Sparse Core Ops, SparseCore 0:
  14.3 30.6 all-gather.4
  46.6 27.3 all-gather.2
  79.6 39.4 all-reduce.2
  250.4 106.0 all-reduce.4
where the time goes:
time: 497 us
  waiting for transfers between devices  298 us (60%)
  blocking collectives  97.6 us (20%)
  matrix products  34.8 us (7%)
  local copies, waits for them, and re-layouts  24.9 us (5%)
  other arithmetic  23.2 us (5%)
  between operations  13.4 us (3%)
  starting transfers between devices  5.24 us (1%)
    psum x2, waiting for transfers between devices, pair_total(): lax.psum(partial_term.astype(jnp.bfloat16), 'pair').astype(jnp.float32)  141 us
    all_to_all x1, blocking collectives, local(): lax.all_to_all(outgoing, 'expert', split_axis=0, concat_axis=0, tiled=True)  97.6 us
    all_to_all x1, waiting for transfers between devices, local(): lax.all_to_all(summed, 'expert', split_axis=0, concat_axis=0, tiled=True)  92.1 us
    all_gather x1, waiting for transfers between devices, local(): shard_keys = lax.all_gather(key_rows, 'expert', axis=0, tiled=True)  26.8 us
    all_gather x1, waiting for transfers between devices, local(): shard_values = lax.all_gather(value_rows, 'expert', axis=0, tiled=True)  22.6 us
    ppermute x1, waiting for transfers between devices, passed_along(): return lax.ppermute(value, axis, pairs)  14.2 us
    dot_general x1, matrix products, local(): lifted = jnp.dot(flat_rows, up_weight, preferred_element_type=jnp.float32)  12.1 us
    reduce_sum x1, other arithmetic, local(): jnp.sum(mix_weights[:, :, None] * returned.astype(jnp.float32), axis=1)  10.1 us
  transfers between devices with their start and end apart: 6, of which 6 were waited for; matrix products, arithmetic and copies ran while one was open for 3% of the time, Pallas kernels for 0%

commit v1 on v0

--- a/solution.py
+++ b/solution.py
@@ -1,9 +1,17 @@
+import functools
+
 import jax
 import jax.numpy as jnp
 from jax import lax
+from jax.experimental import pallas as pl
+from jax.experimental.pallas import tpu as pltpu
 from jax.sharding import PartitionSpec as P
 
+
 BLOCK = 128
+GROUPS = 2
+SMALL_VMEM = 2 << 20
+LARGE_VMEM = 24 << 20
 
 
 def passed_along(value, axis, steps):
@@ -21,7 +29,7 @@
     return lax.psum(partial_term.astype(jnp.bfloat16), "pair").astype(jnp.float32)
 
 
-def local(
+def dispatched(
     tokens, expert_ids, block_mask, attn_gain, w_qkv, w_out, moe_gain, w_router, w_up, w_down
 ):
     rows_here = tokens.shape[0]
@@ -114,6 +122,318 @@
     return passed_along(layer_out, "pipe", 1)
 
 
+def swapped(value, axis, bit):
+    count = lax.axis_size(axis)
+    return lax.ppermute(value, axis, [(source, source ^ bit) for source in range(count)])
+
+
+def doubled(own, axis, skip=0):
+    slots = [own]
+    for slot in range(1, lax.axis_size(axis)):
+        if slot <= skip:
+            slots.append(None)
+        else:
+            slots.append(swapped(slots[slot & (slot - 1)], axis, slot & -slot))
+    return slots
+
+
+def held(value):
+    parts = 4
+    rows = value.shape[0] // parts
+
+    def kernel(source_ref, held_ref, sem):
+        copies = []
+        for part in range(parts):
+            place = pl.ds(part * rows, rows)
+            copies.append(
+                pltpu.make_async_copy(source_ref.at[place], held_ref.at[place], sem.at[part])
+            )
+        for copy in copies:
+            copy.start()
+        for copy in copies:
+            copy.wait()
+
+    return pl.pallas_call(
+        kernel,
+        out_shape=pltpu.VMEM(value.shape, value.dtype),
+        in_specs=[pl.BlockSpec(memory_space=pl.ANY)],
+        out_specs=pl.BlockSpec(memory_space=pltpu.VMEM),
+        scratch_shapes=[pltpu.SemaphoreType.DMA((parts,))],
+        compiler_params=pltpu.CompilerParams(vmem_limit_bytes=SMALL_VMEM),
+    )(value)
+
+
+def attention_kernel(index_ref, mask_ref, query_ref, *refs, score_scale):
+    kv_refs, out_ref = refs[:-1], refs[-1]
+    heads, rows, head_dim = query_ref.shape
+    shard_blocks = rows // BLOCK
+    for head in range(heads):
+        every = []
+        for kv_ref in kv_refs:
+            scores = lax.dot_general(
+                query_ref[head],
+                kv_ref[head, :, :head_dim],
+                (((1,), (1,)), ((), ())),
+                preferred_element_type=jnp.float32,
+            )
+            every.append(scores * score_scale)
+        for block in range(rows // BLOCK):
+            span = slice(block * BLOCK, (block + 1) * BLOCK)
+            masked, flags = [], []
+            for shard, scores in enumerate(every):
+                for part in range(shard_blocks):
+                    flag = mask_ref[block, (index_ref[0] ^ shard) * shard_blocks + part] > 0
+                    piece = scores[span, part * BLOCK : (part + 1) * BLOCK]
+                    masked.append(jnp.where(flag, piece, -1e30))
+                    flags.append(flag)
+            tallest = functools.reduce(jnp.maximum, masked)
+            row_max = jnp.max(tallest, axis=-1, keepdims=True)
+            weights = [
+                jnp.where(flag, jnp.exp(piece - row_max), 0.0)
+                for flag, piece in zip(flags, masked)
+            ]
+            denominator = jnp.sum(functools.reduce(jnp.add, weights), axis=-1, keepdims=True)
+            numerator = jnp.zeros((BLOCK, head_dim), jnp.float32)
+            for shard, kv_ref in enumerate(kv_refs):
+                pieces = weights[shard * shard_blocks : (shard + 1) * shard_blocks]
+                joined = jnp.concatenate(pieces, axis=1).astype(jnp.bfloat16)
+                numerator = numerator + jnp.dot(
+                    joined, kv_ref[head, :, head_dim:], preferred_element_type=jnp.float32
+                )
+            attended = (numerator / denominator).astype(jnp.bfloat16)
+            out_ref[span, head * head_dim : (head + 1) * head_dim] = attended
+
+
+def attention(group, index, mask, queries, kv_own, kv_others):
+    heads, rows, kv_width = kv_others[0].shape
+    head_dim = queries.shape[2]
+    whole_kv = pl.BlockSpec((heads, rows, kv_width), lambda step, *_: (0, 0, 0))
+    return pl.pallas_call(
+        functools.partial(attention_kernel, score_scale=head_dim ** (-0.5)),
+        out_shape=jax.ShapeDtypeStruct((rows, heads * head_dim), jnp.bfloat16),
+        grid_spec=pltpu.PrefetchScalarGridSpec(
+            num_scalar_prefetch=2,
+            grid=(1,),
+            in_specs=[
+                pl.BlockSpec((heads, rows, head_dim), lambda step, *_: (group, 0, 0)),
+                pl.BlockSpec((heads, rows, kv_width), lambda step, *_: (group, 0, 0)),
+            ]
+            + [whole_kv] * len(kv_others),
+            out_specs=pl.BlockSpec((rows, heads * head_dim), lambda step, *_: (0, 0)),
+        ),
+        compiler_params=pltpu.CompilerParams(vmem_limit_bytes=LARGE_VMEM),
+    )(index, mask, queries, kv_own, *kv_others)
+
+
+def blend_kernel(index_ref, *refs, groups, kept):
+    own_refs, other_refs = refs[:groups], refs[groups : 2 * groups]
+    own_out_ref, other_out_ref, stream_ref, gain_ref = refs[2 * groups : 2 * groups + 4]
+    outs = refs[2 * groups + 4 :]
+    half, _ = outs[0].shape
+    side = index_ref[1] if kept else 1 - index_ref[1]
+    rows = pl.ds(pl.multiple_of(side * half, half), half)
+
+    def mixed(part_refs, weight_ref):
+        part = jnp.concatenate([part_ref[rows, :] for part_ref in part_refs], axis=1)
+        total = jnp.dot(part, weight_ref[...], preferred_element_type=jnp.float32)
+        return total.astype(jnp.bfloat16).astype(jnp.float32)
+
+    both = mixed(own_refs, own_out_ref) + mixed(other_refs, other_out_ref)
+    residual = stream_ref[rows, :].astype(jnp.float32) + both
+    normed = rms_scale(residual, gain_ref[...]).astype(jnp.bfloat16)
+    outs[0][...] = normed
+    if kept:
+        quarter = half // 2
+        outs[1][...] = normed[:quarter]
+        outs[2][...] = normed[quarter:]
+        outs[3][...] = residual
+
+
+def blend(index, own_parts, other_parts, own_out, other_out, tokens, gain, kept):
+    rows, model_width = tokens.shape
+    half = rows // 2
+    whole = jax.ShapeDtypeStruct((half, model_width), jnp.bfloat16)
+    part = jax.ShapeDtypeStruct((half // 2, model_width), jnp.bfloat16)
+    residual = jax.ShapeDtypeStruct((half, model_width), jnp.float32)
+    out_shape = (whole, part, part, residual) if kept else (whole,)
+    here = pl.BlockSpec(memory_space=pltpu.VMEM)
+
+    def full(value):
+        return pl.BlockSpec(value.shape, lambda step, index_ref: (0,) * len(value.shape))
+
+    moved = [*own_parts, *other_parts]
+    return pl.pallas_call(
+        functools.partial(blend_kernel, groups=len(own_parts), kept=kept),
+        out_shape=out_shape,
+        grid_spec=pltpu.PrefetchScalarGridSpec(
+            num_scalar_prefetch=1,
+            grid=(1,),
+            in_specs=[full(value) for value in moved] + [here, here, full(tokens), full(gain)],
+            out_specs=tuple(full(value) for value in out_shape),
+        ),
+        compiler_params=pltpu.CompilerParams(vmem_limit_bytes=LARGE_VMEM),
+    )(index, *moved, own_out, other_out, tokens, gain)
+
+
+def largest_tile(extent, most):
+    return max(tile for tile in range(128, most + 1, 128) if extent % tile == 0)
+
+
+def expert_kernel(*refs, pieces):
+    piece_refs = refs[:pieces]
+    up_ref, down_ref, kept_out_ref, given_out_ref, hidden_ref = refs[pieces:]
+    half, width = kept_out_ref.shape
+    hidden_units = up_ref.shape[1]
+    rows = jnp.concatenate([piece_ref[...] for piece_ref in piece_refs], axis=0)
+    tile = largest_tile(hidden_units, 1024)
+    for start in range(0, hidden_units, tile):
+        lifted = jnp.dot(
+            rows, up_ref[:, start : start + tile], preferred_element_type=jnp.float32
+        )
+        hidden = jax.nn.gelu(lifted, approximate=True).astype(jnp.bfloat16)
+        hidden_ref[:, start : start + tile] = hidden
+    tile = largest_tile(width, 512)
+    for start in range(0, width, tile):
+        partial_out = jnp.dot(
+            hidden_ref[...], down_ref[:, start : start + tile], preferred_element_type=jnp.float32
+        ).astype(jnp.bfloat16)
+        kept_out_ref[:, start : start + tile] = partial_out[:half]
+        given_out_ref[:, start : start + tile] = partial_out[half:]
+
+
+def expert_parts(kept, given, up_weight, down_weight):
+    rows = list(kept) + list(given)
+    half = sum(piece.shape[0] for piece in kept)
+    width, hidden_units = up_weight.shape
+    out = jax.ShapeDtypeStruct((half, width), jnp.bfloat16)
+    here = pl.BlockSpec(memory_space=pltpu.VMEM)
+    return pl.pallas_call(
+        functools.partial(expert_kernel, pieces=len(rows)),
+        out_shape=(out, out),
+        grid=(1,),
+        in_specs=[pl.BlockSpec(piece.shape, lambda step: (0, 0)) for piece in rows] + [here] * 2,
+        out_specs=(pl.BlockSpec((half, width), lambda step: (0, 0)),) * 2,
+        scratch_shapes=[pltpu.VMEM((2 * half, hidden_units), jnp.bfloat16)],
+        compiler_params=pltpu.CompilerParams(vmem_limit_bytes=LARGE_VMEM),
+    )(*rows, up_weight, down_weight)
+
+
+def gathered(
+    tokens, expert_ids, block_mask, attn_gain, w_qkv, w_out, moe_gain, w_router, w_up, w_down
+):
+    return section_step(
+        tokens,
+        expert_ids,
+        block_mask,
+        attn_gain,
+        w_qkv,
+        w_out,
+        moe_gain,
+        w_router,
+        w_up,
+        w_down,
+    )
+
+
+def section_step(
+    tokens, expert_ids, block_mask, attn_gain, w_qkv, w_out, moe_gain, w_router, w_up, w_down
+):
+    rows_here, model_width = tokens.shape
+    head_dim = w_qkv.shape[3] // 3
+    experts = lax.axis_size("expert")
+    here = lax.axis_index("expert")
+    side = lax.axis_index("pair")
+    half = rows_here // 2
+    group_heads = w_qkv.shape[2] // GROUPS
+
+    other_out = swapped(w_out[0].reshape(-1, model_width), "pair", 1)
+    normed = rms_scale(tokens, attn_gain[0]).astype(jnp.bfloat16)
+
+    def project(first, last):
+        weight = w_qkv[0, :, :, first * head_dim : last * head_dim]
+        total = jnp.einsum("td,dhc->htc", normed, weight, preferred_element_type=jnp.float32)
+        return total.astype(jnp.bfloat16)
+
+    kv_own = project(1, 3)
+    kv_slots = [
+        doubled(kv_own[group * group_heads : (group + 1) * group_heads], "expert")
+        for group in range(GROUPS)
+    ]
+    queries = project(0, 1)
+    expert_index = jnp.arange(experts, dtype=jnp.int32)
+    one_hot = lax.dynamic_slice_in_dim(expert_ids, side * half, half, 0)[:, :, None] == expert_index
+    slot_here = (expert_index[:, None] ^ here == expert_index).astype(jnp.float32)
+    index = jnp.stack([here, side])
+    up_weight, one_hot, slot_here, index = lax.optimization_barrier(
+        (w_up[0, 0], one_hot.astype(jnp.float32), slot_here, index)
+    )
+    up_held = held(up_weight)
+    down_held = held(w_down[0, 0])
+    attended, other_attended = [], []
+    for group in range(GROUPS):
+        attended.append(attention(group, index, block_mask, queries, kv_own, kv_slots[group][1:]))
+        other_attended.append(swapped(attended[group], "pair", 1))
+    own_held = held(w_out[0].reshape(-1, model_width))
+    other_held = held(other_out)
+
+    def blended(kept):
+        return blend(index, attended, other_attended, own_held, other_held, tokens, moe_gain, kept)
+
+    kept_rows, upper_rows, lower_rows, residual = blended(True)
+    (given_rows,) = blended(False)
+
+    logits = jnp.dot(kept_rows, w_router[0], preferred_element_type=jnp.float32)
+    chosen = jnp.sum(one_hot * logits[:, None, :], axis=-1)
+    gate_values = jax.nn.sigmoid(chosen)
+    mix_weights = gate_values / jnp.sum(gate_values, axis=1, keepdims=True)
+    spread_mix = jnp.sum(one_hot * mix_weights[:, :, None], axis=1)
+
+    upper = doubled(upper_rows, "expert", skip=1)
+    lower = doubled(lower_rows, "expert", skip=1)
+    kept = {0: [kept_rows], 1: [swapped(kept_rows, "expert", 1)]}
+    given = {0: [given_rows], 1: [swapped(given_rows, "expert", 1)]}
+    for slot in range(2, experts):
+        kept[slot] = [upper[slot], lower[slot]]
+        given[slot] = [swapped(upper[slot], "pair", 1), swapped(lower[slot], "pair", 1)]
+    total = residual
+    for slot in range(experts):
+        kept_out, given_out = expert_parts(kept[slot], given[slot], up_held, down_held)
+        received = swapped(given_out, "pair", 1)
+        summed = (kept_out.astype(jnp.float32) + received.astype(jnp.float32)).astype(jnp.bfloat16)
+        if slot:
+            summed = swapped(summed, "expert", slot)
+        column = jnp.sum(spread_mix * slot_here[slot], axis=1, keepdims=True)
+        total = total + column * summed.astype(jnp.float32)
+    layer_out = total.astype(jnp.bfloat16)
+    stages, sides = lax.axis_size("pipe"), lax.axis_size("pair")
+
+    def to_next(flip):
+        pairs = [
+            (stage * sides + place, (stage + 1) % stages * sides + (place ^ flip))
+            for stage in range(stages)
+            for place in range(sides)
+        ]
+        return lax.ppermute(layer_out, ("pipe", "pair"), pairs)
+
+    crossed, straight = to_next(1), to_next(0)
+    first = jnp.where(side == 0, straight, crossed)
+    second = jnp.where(side == 0, crossed, straight)
+    return jnp.concatenate([first, second], axis=0)
+
+
+def local(
+    tokens, expert_ids, block_mask, attn_gain, w_qkv, w_out, moe_gain, w_router, w_up, w_down
+):
+    rows_here = tokens.shape[0]
+    experts = lax.axis_size("expert")
+    capacity = min(rows_here, 2 * rows_here * expert_ids.shape[1] // experts)
+    gathers = capacity == rows_here and lax.axis_size("pair") == 2 and experts & (experts - 1) == 0
+    step = gathered if gathers else dispatched
+    return step(
+        tokens, expert_ids, block_mask, attn_gain, w_qkv, w_out, moe_gain, w_router, w_up, w_down
+    )
+
+
 def solution(mesh):
     return jax.shard_map(
         local,

time: 497 us -> 201 us (0.40)
  the two profiles are of different devices: /device:TPU:0 before, /device:TPU:17 now
where the time goes in v1:
time: 201 us
  waiting for transfers between devices  126 us (63%)
  starting transfers between devices  38.8 us (19%)
  Pallas kernels  27.2 us (14%)
  other arithmetic  4.03 us (2%)
  local copies, waits for them, and re-layouts  2.64 us (1%)
  matrix products  2.3 us (1%)
    ppermute x26, waiting for transfers between devices, swapped(): lax.ppermute(value, axis, [(source, source ^ bit) for source in range(cou...  112 us
    ppermute x26, starting transfers between devices, swapped(): lax.ppermute(value, axis, [(source, source ^ bit) for source in range(cou...  34.6 us
    pallas_call x4, Pallas kernels, expert_parts(): pl.pallas_call(functools.partial(expert_kernel, pieces=len(rows)), out_sh...  17.5 us
    ppermute x2, waiting for transfers between devices, to_next(): return lax.ppermute(layer_out, ('pipe', 'pair'), pairs)  14.2 us
    ppermute x2, starting transfers between devices, to_next(): return lax.ppermute(layer_out, ('pipe', 'pair'), pairs)  4.18 us
  transfers between devices with their start and end apart: 28, of which 18 were waited for; matrix products, arithmetic and copies ran while one was open for 2% of the time, Pallas kernels for 13%

profile of v1, /device:TPU:17, one launch (start us, length us, event | category | flops | bytes accessed | tf_op | source)
XLA Modules:
  0.0 201.1 jit_solution(2689130763187834527)
XLA Ops:
  0.0 1.2 collective-permute-start.8
  1.2 1.5 fusion.1
  2.8 1.2 copy-done.1
  4.0 1.3 slice-done.4
  5.3 1.3 fusion.6.refs_0_
  6.8 1.3 collective-permute-start.3
  8.1 2.3 %collective-permute-start.1 = (bf16[2,256,256]{2,1,0:T(8,128)(2,1)S(1)}, bf16[2,256,256]{2,1,0:T(8,128)(2,1)S(1)}, u32[]{:S(2)}, u32[]{:S(2)}) collective-permute-start(bf16[2,256,256]{2,1,0:T(8,128)(2,1)S(1)} %get-tuple-element.44), channel_id=1, source_target_pairs={{0,4},{2,6},{4,0},{6,2},{1,5},{3,7},{5,1},{7,3},{8,12},{10,14},{12... | collective-permute-start | bytes 786440 | tf_op jit(solution)/shard_map/ppermute | solution.py:127
  10.7 6.7 %collective-permute-done.4.refs_2_ = bf16[2,256,256]{2,1,0:T(8,128)(2,1)S(1)} collective-permute-done((bf16[2,256,256]{2,1,0:T(8,128)(2,1)S(1)}, bf16[2,256,256]{2,1,0:T(8,128)(2,1)S(1)}, u32[]{:S(2)}, u32[]{:S(2)}) %collective-permute-start.4) | collective-permute-done | bytes 262176 | tf_op jit(solution)/shard_map/ppermute | solution.py:127
  17.4 6.5 %collective-permute-start.5 = (bf16[2,256,256]{2,1,0:T(8,128)(2,1)S(1)}, bf16[2,256,256]{2,1,0:T(8,128)(2,1)S(1)}, u32[]{:S(2)}, u32[]{:S(2)}) collective-permute-start(bf16[2,256,256]{2,1,0:T(8,128)(2,1)S(1)} %collective-permute-done.4.refs_2_), channel_id=1, source_target_pairs={{0,2},{2,0},{4,6},{6,4},{1,3},{3,1},{5,7},{7,5},{8,10},{10,8},{12,... | collective-permute-start | bytes 786440 | tf_op jit(solution)/shard_map/ppermute | solution.py:127
  24.0 4.7 %collective-permute-done.1.refs_2_ = bf16[2,256,256]{2,1,0:T(8,128)(2,1)S(1)} collective-permute-done((bf16[2,256,256]{2,1,0:T(8,128)(2,1)S(1)}, bf16[2,256,256]{2,1,0:T(8,128)(2,1)S(1)}, u32[]{:S(2)}, u32[]{:S(2)}) %collective-permute-start.1) | collective-permute-done | bytes 262176 | tf_op jit(solution)/shard_map/ppermute | solution.py:127
  28.7 5.2 %collective-permute-start.2 = (bf16[2,256,256]{2,1,0:T(8,128)(2,1)S(1)}, bf16[2,256,256]{2,1,0:T(8,128)(2,1)S(1)}, u32[]{:S(2)}, u32[]{:S(2)}) collective-permute-start(bf16[2,256,256]{2,1,0:T(8,128)(2,1)S(1)} %collective-permute-done.1.refs_2_), channel_id=1, source_target_pairs={{0,2},{2,0},{4,6},{6,4},{1,3},{3,1},{5,7},{7,5},{8,10},{10,8},{12,... | collective-permute-start | bytes 786440 | tf_op jit(solution)/shard_map/ppermute | solution.py:127
  33.9 0.8 fusion.8.query_ref
  34.7 1.5 collective-permute-done.5.refs_3_
  36.2 1.8 shard_map.101.refs_1_
  38.3 3.5 %collective-permute-done.2.refs_3_ = bf16[2,256,256]{2,1,0:T(8,128)(2,1)S(1)} collective-permute-done((bf16[2,256,256]{2,1,0:T(8,128)(2,1)S(1)}, bf16[2,256,256]{2,1,0:T(8,128)(2,1)S(1)}, u32[]{:S(2)}, u32[]{:S(2)}) %collective-permute-start.2) | collective-permute-done | bytes 262176 | tf_op jit(solution)/shard_map/ppermute | solution.py:127
  41.8 1.8 shard_map.100.refs_0_
  44.1 2.7 %collective-permute-done.8.source_ref = bf16[512,2048]{1,0:T(8,128)(2,1)} collective-permute-done((bf16[512,2048]{1,0:T(8,128)(2,1)}, bf16[512,2048]{1,0:T(8,128)(2,1)}, u32[]{:S(2)}, u32[]{:S(2)}) %collective-permute-start.8) | collective-permute-done | bytes 2097184 | tf_op jit(solution)/shard_map/ppermute | solution.py:127
  46.8 1.7 shard_map.103.refs_5_
  48.6 1.0 collective-permute-done.7.refs_3_
  49.5 2.8 %collective-permute-done.6.refs_2_ = bf16[256,256]{1,0:T(8,128)(2,1)S(1)} collective-permute-done((bf16[256,256]{1,0:T(8,128)(2,1)S(1)}, bf16[256,256]{1,0:T(8,128)(2,1)S(1)}, u32[]{:S(2)}, u32[]{:S(2)}) %collective-permute-start.6) | collective-permute-done | bytes 131104 | tf_op jit(solution)/shard_map/ppermute | solution.py:127
  52.3 1.5 shard_map.104
  54.0 2.3 %collective-permute-start.15 = (bf16[64,2048]{1,0:T(8,128)(2,1)S(1)}, bf16[64,2048]{1,0:T(8,128)(2,1)S(1)}, u32[]{:S(2)}, u32[]{:S(2)}) collective-permute-start(bf16[64,2048]{1,0:T(8,128)(2,1)S(1)} %get-tuple-element.32), channel_id=1, source_target_pairs={{0,4},{2,6},{4,0},{6,2},{1,5},{3,7},{5,1},{7,3},{8,12},{10,14},{12... | collective-permute-start | bytes 786440 | tf_op jit(solution)/shard_map/ppermute | solution.py:127
  56.3 14.0 %collective-permute-done.14.refs_0_ = bf16[64,2048]{1,0:T(8,128)(2,1)S(1)} collective-permute-done((bf16[64,2048]{1,0:T(8,128)(2,1)S(1)}, bf16[64,2048]{1,0:T(8,128)(2,1)S(1)}, u32[]{:S(2)}, u32[]{:S(2)}) %collective-permute-start.14) | collective-permute-done | bytes 262176 | tf_op jit(solution)/shard_map/ppermute | solution.py:127
  70.4 1.1 collective-permute-start.16
  71.5 4.5 %collective-permute-done.15.refs_1_ = bf16[64,2048]{1,0:T(8,128)(2,1)S(1)} collective-permute-done((bf16[64,2048]{1,0:T(8,128)(2,1)S(1)}, bf16[64,2048]{1,0:T(8,128)(2,1)S(1)}, u32[]{:S(2)}, u32[]{:S(2)}) %collective-permute-start.15) | collective-permute-done | bytes 262176 | tf_op jit(solution)/shard_map/ppermute | solution.py:127
  76.0 1.1 collective-permute-start.17
  77.1 1.5 shard_map.105.refs_1_
  78.6 5.3 %collective-permute-start.11 = (bf16[128,2048]{1,0:T(8,128)(2,1)S(1)}, bf16[128,2048]{1,0:T(8,128)(2,1)S(1)}, u32[]{:S(2)}, u32[]{:S(2)}) collective-permute-start(bf16[128,2048]{1,0:T(8,128)(2,1)S(1)} %shard_map.105.refs_1_), channel_id=1, source_target_pairs={{0,2},{2,0},{4,6},{6,4},{1,3},{3,1},{5,7},{7,5},{8,10},{10,8},{12,... | collective-permute-start | bytes 1572872 | tf_op jit(solution)/shard_map/ppermute | solution.py:127
  84.0 1.4 collective-permute-start.20
  86.1 0.7 shard_map.107.refs_3_.refs_5_
  86.8 4.3 %shard_map.110 = (bf16[128,2048]{1,0:T(8,128)(2,1)S(1)}, bf16[128,2048]{1,0:T(8,128)(2,1)S(1)}) custom-call(bf16[64,2048]{1,0:T(8,128)(2,1)S(1)} %collective-permute-done.14.refs_0_, bf16[64,2048]{1,0:T(8,128)(2,1)S(1)} %collective-permute-done.15.refs_1_, bf16[64,2048]{1,0:T(8,128)(2,1)S(1)} %collective-permute-done.16.refs_2_, ...), custom_call_target="tpu_custom_call" | custom-call | tf_op jit(solution)/shard_map/pallas_call | solution.py:310
  91.4 4.3 %shard_map.108 = (bf16[128,2048]{1,0:T(8,128)(2,1)S(1)}, bf16[128,2048]{1,0:T(8,128)(2,1)S(1)}) custom-call(bf16[128,2048]{1,0:T(8,128)(2,1)S(1)} %get-tuple-element.24.refs_0_, bf16[128,2048]{1,0:T(8,128)(2,1)S(1)} %shard_map.105.refs_1_, bf16[2048,1792]{1,0:T(8,128)(2,1)S(1)} %shard_map.106.refs_2_.refs_4_, bf16[1792,2048]{1,0:T(8,128)(2,1)S(1)} %shard_map.107.refs_3_.refs_5_), custom_call_target="tpu_custom_call" | custom-call | tf_op jit(solution)/shard_map/pallas_call | solution.py:310
  95.8 16.5 %collective-permute-done.20.refs_0_ = bf16[64,2048]{1,0:T(8,128)(2,1)S(1)} collective-permute-done((bf16[64,2048]{1,0:T(8,128)(2,1)S(1)}, bf16[64,2048]{1,0:T(8,128)(2,1)S(1)}, u32[]{:S(2)}, u32[]{:S(2)}) %collective-permute-start.20) | collective-permute-done | bytes 262176 | tf_op jit(solution)/shard_map/ppermute | solution.py:127
  112.5 5.4 %collective-permute-done.21.refs_1_ = bf16[64,2048]{1,0:T(8,128)(2,1)S(1)} collective-permute-done((bf16[64,2048]{1,0:T(8,128)(2,1)S(1)}, bf16[64,2048]{1,0:T(8,128)(2,1)S(1)}, u32[]{:S(2)}, u32[]{:S(2)}) %collective-permute-start.21) | collective-permute-done | bytes 262176 | tf_op jit(solution)/shard_map/ppermute | solution.py:127
  118.4 1.3 collective-permute-start.9
  119.6 4.3 %shard_map.109 = (bf16[128,2048]{1,0:T(8,128)(2,1)S(1)}, bf16[128,2048]{1,0:T(8,128)(2,1)S(1)}) custom-call(bf16[128,2048]{1,0:T(8,128)(2,1)S(1)} %collective-permute-done.10.refs_0_, bf16[128,2048]{1,0:T(8,128)(2,1)S(1)} %collective-permute-done.11.refs_1_, bf16[2048,1792]{1,0:T(8,128)(2,1)S(1)} %shard_map.106.refs_2_.refs_4_, ...), custom_call_target="tpu_custom_call" | custom-call | tf_op jit(solution)/shard_map/pallas_call | solution.py:310
  124.4 4.6 %shard_map.111 = (bf16[128,2048]{1,0:T(8,128)(2,1)S(1)}, bf16[128,2048]{1,0:T(8,128)(2,1)S(1)}) custom-call(bf16[64,2048]{1,0:T(8,128)(2,1)S(1)} %collective-permute-done.20.refs_0_, bf16[64,2048]{1,0:T(8,128)(2,1)S(1)} %collective-permute-done.21.refs_1_, bf16[64,2048]{1,0:T(8,128)(2,1)S(1)} %collective-permute-done.22.refs_2_, ...), custom_call_target="tpu_custom_call" | custom-call | tf_op jit(solution)/shard_map/pallas_call | solution.py:310
  129.0 1.2 collective-permute-start.24
  130.4 16.5 %collective-permute-done.12 = bf16[128,2048]{1,0:T(8,128)(2,1)S(1)} collective-permute-done((bf16[128,2048]{1,0:T(8,128)(2,1)S(1)}, bf16[128,2048]{1,0:T(8,128)(2,1)S(1)}, u32[]{:S(2)}, u32[]{:S(2)}) %collective-permute-start.12) | collective-permute-done | bytes 524320 | tf_op jit(solution)/shard_map/ppermute | solution.py:127
  147.0 2.0 collective-permute-start.13
  149.0 9.1 %collective-permute-done.24 = bf16[128,2048]{1,0:T(8,128)(2,1)S(1)} collective-permute-done((bf16[128,2048]{1,0:T(8,128)(2,1)S(1)}, bf16[128,2048]{1,0:T(8,128)(2,1)S(1)}, u32[]{:S(2)}, u32[]{:S(2)}) %collective-permute-start.24) | collective-permute-done | bytes 524320 | tf_op jit(solution)/shard_map/ppermute | solution.py:127
  158.5 19.3 %collective-permute-done.13 = bf16[128,2048]{1,0:T(8,128)(2,1)S(1)} collective-permute-done((bf16[128,2048]{1,0:T(8,128)(2,1)S(1)}, bf16[128,2048]{1,0:T(8,128)(2,1)S(1)}, u32[]{:S(2)}, u32[]{:S(2)}) %collective-permute-start.13) | collective-permute-done | bytes 524320 | tf_op jit(solution)/shard_map/ppermute | solution.py:127
  177.8 3.1 %collective-permute-done.25 = bf16[128,2048]{1,0:T(8,128)(2,1)S(1)} collective-permute-done((bf16[128,2048]{1,0:T(8,128)(2,1)S(1)}, bf16[128,2048]{1,0:T(8,128)(2,1)S(1)}, u32[]{:S(2)}, u32[]{:S(2)}) %collective-permute-start.25) | collective-permute-done | bytes 524320 | tf_op jit(solution)/shard_map/ppermute | solution.py:127
  180.9 0.7 add_convert_fusion
  181.6 4.2 %collective-permute-start.26 = (bf16[128,2048]{1,0:T(8,128)(2,1)S(1)}, bf16[128,2048]{1,0:T(8,128)(2,1)S(1)}, u32[]{:S(2)}, u32[]{:S(2)}) collective-permute-start(bf16[128,2048]{1,0:T(8,128)(2,1)S(1)} %add_convert_fusion), channel_id=1, source_target_pairs={{0,8},{1,9},{8,16},{9,17},{16,24},{17,25},{24,0},{25,1},{2,10},{3,... | collective-permute-start | bytes 1572872 | tf_op jit(solution)/shard_map/ppermute | solution.py:416
  185.7 6.1 %collective-permute-done.26 = bf16[128,2048]{1,0:T(8,128)(2,1)S(1)} collective-permute-done((bf16[128,2048]{1,0:T(8,128)(2,1)S(1)}, bf16[128,2048]{1,0:T(8,128)(2,1)S(1)}, u32[]{:S(2)}, u32[]{:S(2)}) %collective-permute-start.26) | collective-permute-done | bytes 524320 | tf_op jit(solution)/shard_map/ppermute | solution.py:416
  191.9 8.1 %collective-permute-done.27 = bf16[128,2048]{1,0:T(8,128)(2,1)S(1)} collective-permute-done((bf16[128,2048]{1,0:T(8,128)(2,1)S(1)}, bf16[128,2048]{1,0:T(8,128)(2,1)S(1)}, u32[]{:S(2)}, u32[]{:S(2)}) %collective-permute-start.27) | collective-permute-done | bytes 524320 | tf_op jit(solution)/shard_map/ppermute | solution.py:416
  200.0 1.1 pad_maximum_fusion
  (71 shorter events, 4.5 us)
Async XLA Ops:
  0.0 118.1 %copy-start = (bf16[1,2048,4]{1,2,0:T(4,128)(2,1)S(1)}, bf16[1,2048,4]{1,2,0:T(4,128)(2,1)}, u32[]{:S(2)}) copy-start(bf16[1,2048,4]{1,2,0:T(4,128)(2,1)} %param.17) | copy-start | bytes 49156
  0.0 46.8 %collective-permute-start.8 = (bf16[512,2048]{1,0:T(8,128)(2,1)}, bf16[512,2048]{1,0:T(8,128)(2,1)}, u32[]{:S(2)}, u32[]{:S(2)}) collective-permute-start(bf16[512,2048]{1,0:T(8,128)(2,1)} %bitcast.46), channel_id=1, source_target_pairs={{0,1},{1,0},{2,3},{3,2},{4,5},{5,4},{6,7},{7,6},{8,9},{9,8},{10,11... | collective-permute-start | bytes 6291464 | tf_op jit(solution)/shard_map/ppermute | solution.py:127
  2.8 1.2 copy-start.1
  2.8 2.5 %slice-start.4 = ((bf16[1,2048,4,384]{3,2,1,0:T(4,128)(2,1)}), bf16[1,2048,4,256]{3,2,1,0:T(4,128)(2,1)S(1)}, s32[]{:S(2)}) async-start(bf16[1,2048,4,384]{3,2,1,0:T(4,128)(2,1)} %param.14), calls=%async_computation.4 | async-start | bytes 8388608 | tf_op jit(solution)/shard_map/slice | solution.py:353
  2.8 2.5 %copy-start.6 = (f32[1,2048]{1,0:T(1,128)S(1)}, f32[1,2048]{1,0:T(1,128)}, u32[]{:S(2)}) copy-start(f32[1,2048]{1,0:T(1,128)} %param.13) | copy-start | bytes 24580
  5.3 5.3 %copy-start.5 = (s32[256,2]{0,1:T(2,128)S(1)}, s32[256,2]{0,1:T(2,128)}, u32[]{:S(2)}) copy-start(s32[256,2]{0,1:T(2,128)} %param.11) | copy-start | bytes 6148
  6.6 10.8 %collective-permute-start.4 = (bf16[2,256,256]{2,1,0:T(8,128)(2,1)S(1)}, bf16[2,256,256]{2,1,0:T(8,128)(2,1)S(1)}, u32[]{:S(2)}, u32[]{:S(2)}) collective-permute-start(bf16[2,256,256]{2,1,0:T(8,128)(2,1)S(1)} %get-tuple-element.43), channel_id=1, source_target_pairs={{0,4},{2,6},{4,0},{6,2},{1,5},{3,7},{5,1},{7,3},{8,12},{10,14},{12... | collective-permute-start | bytes 786440 | tf_op jit(solution)/shard_map/ppermute | solution.py:127
  6.8 28.0 %collective-permute-start.3 = (bf16[2,256,256]{2,1,0:T(8,128)(2,1)S(1)}, bf16[2,256,256]{2,1,0:T(8,128)(2,1)S(1)}, u32[]{:S(2)}, u32[]{:S(2)}) collective-permute-start(bf16[2,256,256]{2,1,0:T(8,128)(2,1)S(1)} %get-tuple-element.43), channel_id=1, source_target_pairs={{0,2},{2,0},{4,6},{6,4},{1,3},{3,1},{5,7},{7,5},{8,10},{10,8},{12,... | collective-permute-start | bytes 786440 | tf_op jit(solution)/shard_map/ppermute | solution.py:127
  8.1 20.6 %collective-permute-start.1 = (bf16[2,256,256]{2,1,0:T(8,128)(2,1)S(1)}, bf16[2,256,256]{2,1,0:T(8,128)(2,1)S(1)}, u32[]{:S(2)}, u32[]{:S(2)}) collective-permute-start(bf16[2,256,256]{2,1,0:T(8,128)(2,1)S(1)} %get-tuple-element.44), channel_id=1, source_target_pairs={{0,4},{2,6},{4,0},{6,2},{1,5},{3,7},{5,1},{7,3},{8,12},{10,14},{12... | collective-permute-start | bytes 786440 | tf_op jit(solution)/shard_map/ppermute | solution.py:127
  10.4 27.9 %collective-permute-start = (bf16[2,256,256]{2,1,0:T(8,128)(2,1)S(1)}, bf16[2,256,256]{2,1,0:T(8,128)(2,1)S(1)}, u32[]{:S(2)}, u32[]{:S(2)}) collective-permute-start(bf16[2,256,256]{2,1,0:T(8,128)(2,1)S(1)} %get-tuple-element.44), channel_id=1, source_target_pairs={{0,2},{2,0},{4,6},{6,4},{1,3},{3,1},{5,7},{7,5},{8,10},{10,8},{12,... | collective-permute-start | bytes 786440 | tf_op jit(solution)/shard_map/ppermute | solution.py:127
  10.7 23.3 %slice-start.5 = ((bf16[1,2048,4,384]{3,2,1,0:T(4,128)(2,1)}), bf16[1,2048,4,128]{3,2,1,0:T(4,128)(2,1)S(1)}, s32[]{:S(2)}) async-start(bf16[1,2048,4,384]{3,2,1,0:T(4,128)(2,1)} %param.14), calls=%async_computation.5 | async-start | bytes 4194304 | tf_op jit(solution)/shard_map/slice | solution.py:353
  10.7 25.5 %copy-start.4 = (s32[2,8]{1,0:T(2,128)S(1)}, s32[2,8]{1,0:T(2,128)}, u32[]{:S(2)}) copy-start(s32[2,8]{1,0:T(2,128)} %mask_ref.3) | copy-start | bytes 196
  17.4 18.8 %collective-permute-start.5 = (bf16[2,256,256]{2,1,0:T(8,128)(2,1)S(1)}, bf16[2,256,256]{2,1,0:T(8,128)(2,1)S(1)}, u32[]{:S(2)}, u32[]{:S(2)}) collective-permute-start(bf16[2,256,256]{2,1,0:T(8,128)(2,1)S(1)} %collective-permute-done.4.refs_2_), channel_id=1, source_target_pairs={{0,2},{2,0},{4,6},{6,4},{1,3},{3,1},{5,7},{7,5},{8,10},{10,8},{12,... | collective-permute-start | bytes 786440 | tf_op jit(solution)/shard_map/ppermute | solution.py:127
  28.7 13.1 %collective-permute-start.2 = (bf16[2,256,256]{2,1,0:T(8,128)(2,1)S(1)}, bf16[2,256,256]{2,1,0:T(8,128)(2,1)S(1)}, u32[]{:S(2)}, u32[]{:S(2)}) collective-permute-start(bf16[2,256,256]{2,1,0:T(8,128)(2,1)S(1)} %collective-permute-done.1.refs_2_), channel_id=1, source_target_pairs={{0,2},{2,0},{4,6},{6,4},{1,3},{3,1},{5,7},{7,5},{8,10},{10,8},{12,... | collective-permute-start | bytes 786440 | tf_op jit(solution)/shard_map/ppermute | solution.py:127
  34.7 9.2 %copy-start.2 = (bf16[1,4,128,2048]{3,2,1,0:T(8,128)(2,1)S(1)}, bf16[1,4,128,2048]{3,2,1,0:T(8,128)(2,1)}, u32[]{:S(2)}) copy-start(bf16[1,4,128,2048]{3,2,1,0:T(8,128)(2,1)} %param.15) | copy-start | bytes 6291460
  38.0 11.5 %collective-permute-start.7 = (bf16[256,256]{1,0:T(8,128)(2,1)S(1)}, bf16[256,256]{1,0:T(8,128)(2,1)S(1)}, u32[]{:S(2)}, u32[]{:S(2)}) collective-permute-start(bf16[256,256]{1,0:T(8,128)(2,1)S(1)} %shard_map.101.refs_1_), channel_id=1, source_target_pairs={{0,1},{1,0},{2,3},{3,2},{4,5},{5,4},{6,7},{7,6},{8,9},{9,8},{10,11... | collective-permute-start | bytes 393224 | tf_op jit(solution)/shard_map/ppermute | solution.py:127
  43.6 8.7 %collective-permute-start.6 = (bf16[256,256]{1,0:T(8,128)(2,1)S(1)}, bf16[256,256]{1,0:T(8,128)(2,1)S(1)}, u32[]{:S(2)}, u32[]{:S(2)}) collective-permute-start(bf16[256,256]{1,0:T(8,128)(2,1)S(1)} %shard_map.100.refs_0_), channel_id=1, source_target_pairs={{0,1},{1,0},{2,3},{3,2},{4,5},{5,4},{6,7},{7,6},{8,9},{9,8},{10,11... | collective-permute-start | bytes 393224 | tf_op jit(solution)/shard_map/ppermute | solution.py:127
  44.1 8.2 %copy-start.3 = (f32[1,2048]{1,0:T(1,128)S(1)}, f32[1,2048]{1,0:T(1,128)}, u32[]{:S(2)}) copy-start(f32[1,2048]{1,0:T(1,128)} %refs_7_.3) | copy-start | bytes 24580
  46.8 38.6 %slice-start = ((s8[7340032]{0:T(1024)(128)(4,1)}), s8[4194304]{0:T(1024)(128)(4,1)S(1)}, s32[]{:S(2)}) async-start(s8[7340032]{0:T(1024)(128)(4,1)} %bitcast.40), calls=%async_computation | async-start | bytes 8388608
  48.5 36.9 %slice-start.1 = ((s8[7340032]{0:T(1024)(128)(4,1)}), s8[3145728]{0:T(1024)(128)(4,1)S(1)}, s32[]{:S(2)}) async-start(s8[7340032]{0:T(1024)(128)(4,1)} %bitcast.40), calls=%async_computation.1 | async-start | bytes 6291456
  53.9 16.5 %collective-permute-start.14 = (bf16[64,2048]{1,0:T(8,128)(2,1)S(1)}, bf16[64,2048]{1,0:T(8,128)(2,1)S(1)}, u32[]{:S(2)}, u32[]{:S(2)}) collective-permute-start(bf16[64,2048]{1,0:T(8,128)(2,1)S(1)} %get-tuple-element.31), channel_id=1, source_target_pairs={{0,4},{2,6},{4,0},{6,2},{1,5},{3,7},{5,1},{7,3},{8,12},{10,14},{12... | collective-permute-start | bytes 786440 | tf_op jit(solution)/shard_map/ppermute | solution.py:127
  54.0 21.9 %collective-permute-start.15 = (bf16[64,2048]{1,0:T(8,128)(2,1)S(1)}, bf16[64,2048]{1,0:T(8,128)(2,1)S(1)}, u32[]{:S(2)}, u32[]{:S(2)}) collective-permute-start(bf16[64,2048]{1,0:T(8,128)(2,1)S(1)} %get-tuple-element.32), channel_id=1, source_target_pairs={{0,4},{2,6},{4,0},{6,2},{1,5},{3,7},{5,1},{7,3},{8,12},{10,14},{12... | collective-permute-start | bytes 786440 | tf_op jit(solution)/shard_map/ppermute | solution.py:127
  70.4 15.0 %collective-permute-start.16 = (bf16[64,2048]{1,0:T(8,128)(2,1)S(1)}, bf16[64,2048]{1,0:T(8,128)(2,1)S(1)}, u32[]{:S(2)}, u32[]{:S(2)}) collective-permute-start(bf16[64,2048]{1,0:T(8,128)(2,1)S(1)} %collective-permute-done.14.refs_0_), channel_id=1, source_target_pairs={{0,1},{1,0},{2,3},{3,2},{4,5},{5,4},{6,7},{7,6},{8,9},{9,8},{10,11... | collective-permute-start | bytes 786440 | tf_op jit(solution)/shard_map/ppermute | solution.py:127
  76.0 10.8 %collective-permute-start.17 = (bf16[64,2048]{1,0:T(8,128)(2,1)S(1)}, bf16[64,2048]{1,0:T(8,128)(2,1)S(1)}, u32[]{:S(2)}, u32[]{:S(2)}) collective-permute-start(bf16[64,2048]{1,0:T(8,128)(2,1)S(1)} %collective-permute-done.15.refs_1_), channel_id=1, source_target_pairs={{0,1},{1,0},{2,3},{3,2},{4,5},{5,4},{6,7},{7,6},{8,9},{9,8},{10,11... | collective-permute-start | bytes 786440 | tf_op jit(solution)/shard_map/ppermute | solution.py:127
  77.1 8.9 %slice-start.2 = ((s8[7340032]{0:T(1024)(128)(4,1)}), s8[3145728]{0:T(1024)(128)(4,1)S(1)}, s32[]{:S(2)}) async-start(s8[7340032]{0:T(1024)(128)(4,1)} %bitcast.43), calls=%async_computation.2 | async-start | bytes 6291456
  78.6 39.8 %collective-permute-start.11 = (bf16[128,2048]{1,0:T(8,128)(2,1)S(1)}, bf16[128,2048]{1,0:T(8,128)(2,1)S(1)}, u32[]{:S(2)}, u32[]{:S(2)}) collective-permute-start(bf16[128,2048]{1,0:T(8,128)(2,1)S(1)} %shard_map.105.refs_1_), channel_id=1, source_target_pairs={{0,2},{2,0},{4,6},{6,4},{1,3},{3,1},{5,7},{7,5},{8,10},{10,8},{12,... | collective-permute-start | bytes 1572872 | tf_op jit(solution)/shard_map/ppermute | solution.py:127
  83.9 2.2 %slice-start.3 = ((s8[7340032]{0:T(1024)(128)(4,1)}), s8[4194304]{0:T(1024)(128)(4,1)S(1)}, s32[]{:S(2)}) async-start(s8[7340032]{0:T(1024)(128)(4,1)} %bitcast.43), calls=%async_computation.3 | async-start | bytes 8388608
  83.9 35.7 %collective-permute-start.10 = (bf16[128,2048]{1,0:T(8,128)(2,1)S(1)}, bf16[128,2048]{1,0:T(8,128)(2,1)S(1)}, u32[]{:S(2)}, u32[]{:S(2)}) collective-permute-start(bf16[128,2048]{1,0:T(8,128)(2,1)S(1)} %get-tuple-element.24.refs_0_), channel_id=1, source_target_pairs={{0,2},{2,0},{4,6},{6,4},{1,3},{3,1},{5,7},{7,5},{8,10},{10,8},{12,... | collective-permute-start | bytes 1572872 | tf_op jit(solution)/shard_map/ppermute | solution.py:127
  84.0 28.3 %collective-permute-start.20 = (bf16[64,2048]{1,0:T(8,128)(2,1)S(1)}, bf16[64,2048]{1,0:T(8,128)(2,1)S(1)}, u32[]{:S(2)}, u32[]{:S(2)}) collective-permute-start(bf16[64,2048]{1,0:T(8,128)(2,1)S(1)} %collective-permute-done.14.refs_0_), channel_id=1, source_target_pairs={{0,2},{2,0},{4,6},{6,4},{1,3},{3,1},{5,7},{7,5},{8,10},{10,8},{12,... | collective-permute-start | bytes 786440 | tf_op jit(solution)/shard_map/ppermute | solution.py:127
  85.4 32.5 %collective-permute-start.21 = (bf16[64,2048]{1,0:T(8,128)(2,1)S(1)}, bf16[64,2048]{1,0:T(8,128)(2,1)S(1)}, u32[]{:S(2)}, u32[]{:S(2)}) collective-permute-start(bf16[64,2048]{1,0:T(8,128)(2,1)S(1)} %collective-permute-done.15.refs_1_), channel_id=1, source_target_pairs={{0,2},{2,0},{4,6},{6,4},{1,3},{3,1},{5,7},{7,5},{8,10},{10,8},{12,... | collective-permute-start | bytes 786440 | tf_op jit(solution)/shard_map/ppermute | solution.py:127
  91.1 39.0 %collective-permute-start.18 = (bf16[128,2048]{1,0:T(8,128)(2,1)S(1)}, bf16[128,2048]{1,0:T(8,128)(2,1)S(1)}, u32[]{:S(2)}, u32[]{:S(2)}) collective-permute-start(bf16[128,2048]{1,0:T(8,128)(2,1)S(1)} %get-tuple-element.34), channel_id=1, source_target_pairs={{0,1},{1,0},{2,3},{3,2},{4,5},{5,4},{6,7},{7,6},{8,9},{9,8},{10,11... | collective-permute-start | bytes 1572872 | tf_op jit(solution)/shard_map/ppermute | solution.py:127
  112.3 12.0 %collective-permute-start.22 = (bf16[64,2048]{1,0:T(8,128)(2,1)S(1)}, bf16[64,2048]{1,0:T(8,128)(2,1)S(1)}, u32[]{:S(2)}, u32[]{:S(2)}) collective-permute-start(bf16[64,2048]{1,0:T(8,128)(2,1)S(1)} %collective-permute-done.20.refs_0_), channel_id=1, source_target_pairs={{0,1},{1,0},{2,3},{3,2},{4,5},{5,4},{6,7},{7,6},{8,9},{9,8},{10,11... | collective-permute-start | bytes 786440 | tf_op jit(solution)/shard_map/ppermute | solution.py:127
  117.9 6.5 %collective-permute-start.23 = (bf16[64,2048]{1,0:T(8,128)(2,1)S(1)}, bf16[64,2048]{1,0:T(8,128)(2,1)S(1)}, u32[]{:S(2)}, u32[]{:S(2)}) collective-permute-start(bf16[64,2048]{1,0:T(8,128)(2,1)S(1)} %collective-permute-done.21.refs_1_), channel_id=1, source_target_pairs={{0,1},{1,0},{2,3},{3,2},{4,5},{5,4},{6,7},{7,6},{8,9},{9,8},{10,11... | collective-permute-start | bytes 786440 | tf_op jit(solution)/shard_map/ppermute | solution.py:127
  118.4 40.1 %collective-permute-start.9 = (bf16[128,2048]{1,0:T(8,128)(2,1)S(1)}, bf16[128,2048]{1,0:T(8,128)(2,1)S(1)}, u32[]{:S(2)}, u32[]{:S(2)}) collective-permute-start(bf16[128,2048]{1,0:T(8,128)(2,1)S(1)} %get-tuple-element.28), channel_id=1, source_target_pairs={{0,1},{1,0},{2,3},{3,2},{4,5},{5,4},{6,7},{7,6},{8,9},{9,8},{10,11... | collective-permute-start | bytes 1572872 | tf_op jit(solution)/shard_map/ppermute | solution.py:127
  124.0 22.9 %collective-permute-start.12 = (bf16[128,2048]{1,0:T(8,128)(2,1)S(1)}, bf16[128,2048]{1,0:T(8,128)(2,1)S(1)}, u32[]{:S(2)}, u32[]{:S(2)}) collective-permute-start(bf16[128,2048]{1,0:T(8,128)(2,1)S(1)} %get-tuple-element.30), channel_id=1, source_target_pairs={{0,1},{1,0},{2,3},{3,2},{4,5},{5,4},{6,7},{7,6},{8,9},{9,8},{10,11... | collective-permute-start | bytes 1572872 | tf_op jit(solution)/shard_map/ppermute | solution.py:127
  129.0 29.1 %collective-permute-start.24 = (bf16[128,2048]{1,0:T(8,128)(2,1)S(1)}, bf16[128,2048]{1,0:T(8,128)(2,1)S(1)}, u32[]{:S(2)}, u32[]{:S(2)}) collective-permute-start(bf16[128,2048]{1,0:T(8,128)(2,1)S(1)} %get-tuple-element.36), channel_id=1, source_target_pairs={{0,1},{1,0},{2,3},{3,2},{4,5},{5,4},{6,7},{7,6},{8,9},{9,8},{10,11... | collective-permute-start | bytes 1572872 | tf_op jit(solution)/shard_map/ppermute | solution.py:127
  130.3 28.2 %collective-permute-start.19 = (bf16[128,2048]{1,0:T(8,128)(2,1)S(1)}, bf16[128,2048]{1,0:T(8,128)(2,1)S(1)}, u32[]{:S(2)}, u32[]{:S(2)}) collective-permute-start(bf16[128,2048]{1,0:T(8,128)(2,1)S(1)} %add_convert_fusion.2), channel_id=1, source_target_pairs={{0,4},{2,6},{4,0},{6,2},{1,5},{3,7},{5,1},{7,3},{8,12},{10,14},{12... | collective-permute-start | bytes 1572872 | tf_op jit(solution)/shard_map/ppermute | solution.py:127
  147.0 30.8 %collective-permute-start.13 = (bf16[128,2048]{1,0:T(8,128)(2,1)S(1)}, bf16[128,2048]{1,0:T(8,128)(2,1)S(1)}, u32[]{:S(2)}, u32[]{:S(2)}) collective-permute-start(bf16[128,2048]{1,0:T(8,128)(2,1)S(1)} %add_convert_fusion.3), channel_id=1, source_target_pairs={{0,2},{2,0},{4,6},{6,4},{1,3},{3,1},{5,7},{7,5},{8,10},{10,8},{12,... | collective-permute-start | bytes 1572872 | tf_op jit(solution)/shard_map/ppermute | solution.py:127
  158.3 22.6 %collective-permute-start.25 = (bf16[128,2048]{1,0:T(8,128)(2,1)S(1)}, bf16[128,2048]{1,0:T(8,128)(2,1)S(1)}, u32[]{:S(2)}, u32[]{:S(2)}) collective-permute-start(bf16[128,2048]{1,0:T(8,128)(2,1)S(1)} %add_convert_fusion.1), channel_id=1, source_target_pairs={{0,6},{2,4},{4,2},{6,0},{1,7},{3,5},{5,3},{7,1},{8,14},{10,12},{12... | collective-permute-start | bytes 1572872 | tf_op jit(solution)/shard_map/ppermute | solution.py:127
  181.6 10.3 %collective-permute-start.26 = (bf16[128,2048]{1,0:T(8,128)(2,1)S(1)}, bf16[128,2048]{1,0:T(8,128)(2,1)S(1)}, u32[]{:S(2)}, u32[]{:S(2)}) collective-permute-start(bf16[128,2048]{1,0:T(8,128)(2,1)S(1)} %add_convert_fusion), channel_id=1, source_target_pairs={{0,8},{1,9},{8,16},{9,17},{16,24},{17,25},{24,0},{25,1},{2,10},{3,... | collective-permute-start | bytes 1572872 | tf_op jit(solution)/shard_map/ppermute | solution.py:416
  185.7 14.2 %collective-permute-start.27 = (bf16[128,2048]{1,0:T(8,128)(2,1)S(1)}, bf16[128,2048]{1,0:T(8,128)(2,1)S(1)}, u32[]{:S(2)}, u32[]{:S(2)}) collective-permute-start(bf16[128,2048]{1,0:T(8,128)(2,1)S(1)} %add_convert_fusion), channel_id=1, source_target_pairs={{0,9},{1,8},{8,17},{9,16},{16,25},{17,24},{24,1},{25,0},{2,11},{3,... | collective-permute-start | bytes 1572872 | tf_op jit(solution)/shard_map/ppermute | solution.py:416
